TPU v7x, 128 devices: a whole 4x4x4 slice. The times are simulated.
128 devices in a mesh: leaf: 16 (over x, z), row: 8 (over y, core).
Axes of the slice: x: 4, y: 4, z: 4, core: 2. Of those that a mesh axis runs over, the one named last changes fastest.
Arguments:
- right_side: float32 [16, 2048, 1024], P('leaf', 'row'), may hold values from -6 to 6
- lower_rows: float32 [16, 2048, 2048], P('leaf', 'row'), may hold values from -0.125 to 0.125
- diag_inverse: float32 [16, 2048, 256], P('leaf', 'row'), may hold values from -0.375 to 0.375
- update_rows: float32 [16, 4096, 2048], P('leaf', 'row'), may hold values from -0.125 to 0.125
- owner_map: int32 [16, 32], P('leaf', 'row'), may hold values from 0 to 127, as said below
- block_counts: int32 [16], P('leaf'), may hold values from 1 to 32, as said below
- ancestor_rhs: float32 [16, 8192, 1024], P('leaf', 'row'), may hold values from -6 to 6
- ancestor_inverse: float32 [16, 8192, 128], P('leaf', 'row'), may hold values from -0.5 to 0.5
Outputs:
- solution: float32 [16, 2048, 1024], P('leaf', 'row')
- parent_front_solution_rows: float32 [16, 8192, 1024], P('leaf', 'row')
Inputs may be any that keep to these rules, and one draw needn't show every extreme that they name: `owner_map`: among the 4 blocks b with the same b // 4 of one front, the values g // 8 are distinct. `block_counts`: some front has all its blocks live.
All inputs are finite; a program needn't handle non-finite values.
Results may differ from a plain program's by a relative error of at most 0.0001.
Values sent between devices are 32-bit elements; how exact they have to be, the bound alone decides.
A program may use at most 320 MiB of HBM per device.

v0:
```python
import jax
import jax.numpy as jnp
from jax import lax
from jax.sharding import PartitionSpec as P

BLK = 128


def spread(value, axis, source):
    kept = jnp.where(lax.axis_index(axis) == source, value, 0).astype(value.dtype)
    return lax.psum(kept, axis)


def body(
    right_side,
    lower_rows,
    diag_inverse,
    update_rows,
    owner_map,
    block_counts,
    ancestor_rhs,
    ancestor_inverse,
):
    topmost_front = lax.Precision.HIGHEST
    n_row = lax.axis_size("row")
    n_leaf = lax.axis_size("leaf")
    my_row = lax.axis_index("row")
    rhs_own = right_side[0]
    lower = lower_rows[0]
    inverse = diag_inverse[0]
    update_blocks = update_rows[0]
    panel = rhs_own.shape[0]
    columns = rhs_own.shape[1]
    accum = jnp.zeros((panel, columns), jnp.float32)
    solution = jnp.zeros((panel, columns), jnp.float32)
    update_sum = jnp.zeros((update_blocks.shape[0], columns), jnp.float32)
    for step in range(n_row):
        proposed_front = jnp.dot(
            inverse, rhs_own - accum, precision=topmost_front, preferred_element_type=jnp.float32
        )
        received_contribution = spread(proposed_front, "row", step)
        solution = jnp.where(my_row == step, received_contribution, solution)
        if step + 1 < n_row:
            accum = accum + jnp.dot(
                lower[:, step * panel : (step + 1) * panel],
                received_contribution,
                precision=topmost_front,
                preferred_element_type=jnp.float32,
            )
        update_sum = update_sum + jnp.dot(
            update_blocks[:, step * panel : (step + 1) * panel],
            received_contribution,
            precision=topmost_front,
            preferred_element_type=jnp.float32,
        )
    nblocks = update_blocks.shape[0] // BLK
    blocks = update_sum.reshape(nblocks, BLK, columns)
    targets_per = ancestor_rhs.shape[1] // BLK
    global_index = my_row * nblocks + jnp.arange(nblocks, dtype=jnp.int32)
    live = (global_index < block_counts[0]).astype(jnp.float32)
    targets = owner_map[0]
    table = (targets[:, None] == jnp.arange(n_leaf * targets_per, dtype=jnp.int32)[None]).astype(
        jnp.float32
    ) * live[:, None]
    broadcast_rows = jnp.einsum("ug,ubc->gbc", table, blocks, precision=topmost_front)
    summed = lax.psum_scatter(broadcast_rows, "leaf", scatter_dimension=0, tiled=True)
    remaining_right_side = ancestor_rhs[0].reshape(targets_per, BLK, columns) - summed
    inverted_diagonal_block = ancestor_inverse[0].reshape(targets_per, BLK, BLK)
    parent_front_solution_rows = jnp.einsum(
        "usq,uqp->usp", inverted_diagonal_block, remaining_right_side, precision=topmost_front
    )
    return (solution[None], parent_front_solution_rows.reshape(1, targets_per * BLK, columns))


def solution(mesh):
    in_specs = (
        P("leaf", "row", None),
        P("leaf", "row", None),
        P("leaf", "row", None),
        P("leaf", "row", None),
        P("leaf", "row"),
        P("leaf"),
        P("leaf", "row", None),
        P("leaf", "row", None),
    )
    out_specs = (P("leaf", "row", None), P("leaf", "row", None))
    return jax.shard_map(body, mesh=mesh, in_specs=in_specs, out_specs=out_specs, check_vma=False)
```

profile of v0, /device:TPU:8, one launch (start us, length us, event | category | flops | bytes accessed | tf_op | source)
XLA Modules:
  0.0 1056.8 jit_solution(11400715886202516422)
XLA Ops:
  11.1 62.5 %all-reduce.9.cloned.1.call-done = f32[256,1024]{1,0:T(8,128)} async-done(((f32[256,1024]{1,0:T(8,128)}), f32[256,1024]{1,0:T(8,128)}) %all-reduce.9.cloned.1.call-update) | async-done | bytes 1048592 | tf_op jit(solution)/shard_map/psum | solution.py:11
  79.8 62.2 %all-reduce.11.cloned.1.call-done = f32[256,1024]{1,0:T(8,128)} async-done(((f32[256,1024]{1,0:T(8,128)}), f32[256,1024]{1,0:T(8,128)}) %all-reduce.11.cloned.1.call-update) | async-done | bytes 1048592 | tf_op jit(solution)/shard_map/psum | solution.py:11
  142.0 3.4 fusion.11
  147.6 62.2 %all-reduce.13.cloned.1.call-done = f32[256,1024]{1,0:T(8,128)} async-done(((f32[256,1024]{1,0:T(8,128)}), f32[256,1024]{1,0:T(8,128)}) %all-reduce.13.cloned.1.call-update) | async-done | bytes 1048592 | tf_op jit(solution)/shard_map/psum | solution.py:11
  216.2 62.0 %all-reduce.15.cloned.1.call-done = f32[256,1024]{1,0:T(8,128)} async-done(((f32[256,1024]{1,0:T(8,128)}), f32[256,1024]{1,0:T(8,128)}) %all-reduce.15.cloned.1.call-update) | async-done | bytes 1048592 | tf_op jit(solution)/shard_map/psum | solution.py:11
  278.2 3.4 fusion.13
  285.4 4.2 fusion.32
  289.7 57.3 %all-reduce.17.cloned.1.call-done = f32[256,1024]{1,0:T(8,128)} async-done(((f32[256,1024]{1,0:T(8,128)}), f32[256,1024]{1,0:T(8,128)}) %all-reduce.17.cloned.1.call-update) | async-done | bytes 1048592 | tf_op jit(solution)/shard_map/psum | solution.py:11
  353.7 4.7 fusion.30
  358.4 4.2 fusion.28
  362.6 53.1 %all-reduce.19.cloned.1.call-done = f32[256,1024]{1,0:T(8,128)} async-done(((f32[256,1024]{1,0:T(8,128)}), f32[256,1024]{1,0:T(8,128)}) %all-reduce.19.cloned.1.call-update) | async-done | bytes 1048592 | tf_op jit(solution)/shard_map/psum | solution.py:11
  415.7 3.4 fusion.15
  422.5 4.7 fusion.26
  427.2 4.3 fusion.24
  431.4 53.0 %all-reduce.21.cloned.1.call-done = f32[256,1024]{1,0:T(8,128)} async-done(((f32[256,1024]{1,0:T(8,128)}), f32[256,1024]{1,0:T(8,128)}) %all-reduce.21.cloned.1.call-update) | async-done | bytes 1048592 | tf_op jit(solution)/shard_map/psum | solution.py:11
  484.4 3.4 fusion.17
  490.5 4.6 fusion.22
  495.0 4.2 fusion.20
  499.3 52.9 %all-reduce.23.cloned.1.call-done = f32[256,1024]{1,0:T(8,128)} async-done(((f32[256,1024]{1,0:T(8,128)}), f32[256,1024]{1,0:T(8,128)}) %all-reduce.23.cloned.1.call-update) | async-done | bytes 1048592 | tf_op jit(solution)/shard_map/psum | solution.py:11
  552.2 8.2 add_add_fusion
  560.4 58.0 %fusion.2 = f32[128,128,1024]{2,0,1:T(8,128)} fusion(f32[4,128,1024]{2,1,0:T(8,128)S(1)} %bitcast.114, f32[4]{0:T(128)S(1)} %compare_convert_fusion, s32[4]{0:T(128)S(1)} %bitcast.132), kind=kOutput, calls=%fused_computation.2 | convolution fusion | flops 805307392 | bytes 69206048 | tf_op jit(solution)/shard_map/ug,ubc->gbc/dot_general | solution.py:65
  618.4 56.5 %copy.26 = f32[128,128,1024]{2,1,0:T(8,128)} copy(f32[128,128,1024]{2,0,1:T(8,128)} %fusion.2) | data formatting | bytes 134217728 | tf_op jit(solution)/shard_map/ug,ubc->gbc/dot_general | solution.py:65
  678.2 362.5 %reduce-scatter.2.cloned.1.call-done = f32[8,128,1024]{2,1,0:T(8,128)} async-done(((f32[128,128,1024]{2,1,0:T(8,128)}), f32[8,128,1024]{2,1,0:T(8,128)}) %reduce-scatter.2.cloned.1.call-update) | async-done | bytes 4194320 | tf_op jit(solution)/shard_map/reduce_scatter | solution.py:66
  1040.7 9.4 fusion
  (58 shorter events, 37.6 us)
Async XLA Ops:
  7.2 1033.5 %copy-start = (f32[1,1024,128]{2,1,0:T(8,128)S(1)}, f32[1,1024,128]{2,1,0:T(8,128)}, u32[]{:S(2)}) copy-start(f32[1,1024,128]{2,1,0:T(8,128)} %param.15) | copy-start | bytes 1572868
  7.2 3.6 copy-start.11
  7.2 66.4 %all-reduce.9.cloned.1.call-start = ((), (), s32[]{:S(2)}) async-start(), calls=%async_computation.1 | async-start | bytes 2097152 | tf_op jit(solution)/shard_map/psum | solution.py:11
  10.7 67.0 %copy-start.1 = (f32[1,256,256]{2,1,0:T(8,128)S(1)}, f32[1,256,256]{2,1,0:T(8,128)}, u32[]{:S(2)}) copy-start(f32[1,256,256]{2,1,0:T(8,128)} %param.10) | copy-start | bytes 786436
  10.7 131.3 %all-reduce.11.cloned.1.call-start = ((), (), s32[]{:S(2)}) async-start(), calls=%async_computation.2 | async-start | bytes 2097152 | tf_op jit(solution)/shard_map/psum | solution.py:11
  76.7 1.0 copy-start.9
  79.8 130.0 %all-reduce.13.cloned.1.call-start = ((), (), s32[]{:S(2)}) async-start(), calls=%async_computation.3 | async-start | bytes 2097152 | tf_op jit(solution)/shard_map/psum | solution.py:11
  147.6 130.6 %all-reduce.15.cloned.1.call-start = ((), (), s32[]{:S(2)}) async-start(), calls=%async_computation.4 | async-start | bytes 2097152 | tf_op jit(solution)/shard_map/psum | solution.py:11
  212.9 1.0 copy-start.10
  215.9 131.0 %all-reduce.17.cloned.1.call-start = ((), (), s32[]{:S(2)}) async-start(), calls=%async_computation.5 | async-start | bytes 2097152 | tf_op jit(solution)/shard_map/psum | solution.py:11
  281.6 1.0 copy-start.7
  282.6 2.8 copy-start.3
  284.7 131.0 %all-reduce.19.cloned.1.call-start = ((), (), s32[]{:S(2)}) async-start(), calls=%async_computation.6 | async-start | bytes 2097152 | tf_op jit(solution)/shard_map/psum | solution.py:11
  350.4 1.0 copy-start.8
  353.4 131.0 %all-reduce.21.cloned.1.call-start = ((), (), s32[]{:S(2)}) async-start(), calls=%async_computation.7 | async-start | bytes 2097152 | tf_op jit(solution)/shard_map/psum | solution.py:11
  353.7 4.7 copy-start.4
  419.1 1.0 copy-start.6
  422.2 130.0 %all-reduce.23.cloned.1.call-start = ((), (), s32[]{:S(2)}) async-start(), calls=%async_computation.8 | async-start | bytes 2097152 | tf_op jit(solution)/shard_map/psum | solution.py:11
  422.5 4.7 copy-start.5
  489.9 5.1 copy-start.2
  489.9 550.7 %reduce-scatter.2.cloned.1.call-start = ((), (), s32[]{:S(2)}) async-start(), calls=%async_computation.9 | async-start | bytes 71303168 | tf_op jit(solution)/shard_map/reduce_scatter | solution.py:66
  499.3 61.1 %copy-start.12 = (s32[1,4]{1,0:T(1,128)S(1)}, s32[1,4]{1,0:T(1,128)}, u32[]{:S(2)}) copy-start(s32[1,4]{1,0:T(1,128)} %param.12) | copy-start | bytes 52
Sparse Core Ops, SparseCore 0:
  10.9 62.6 all-reduce.8
  79.9 62.0 all-reduce.10
  147.7 62.0 all-reduce.12
  216.1 62.0 all-reduce.14
  284.8 62.0 all-reduce.16
  353.6 62.0 all-reduce.18
  422.3 62.0 all-reduce.20
  490.1 62.0 all-reduce.22
  675.1 365.4 reduce-scatter.1
where the time goes:
time: 1070 us; the launch traced here: 1060 us
  waiting for transfers between devices  828 us (77%)
  matrix products  148 us (14%)
  local copies, waits for them, and re-layouts  61.7 us (6%)
  between operations  15 us (1%)
    psum x8, waiting for transfers between devices, spread(): return lax.psum(kept, axis)  465 us
    reduce_scatter x1, waiting for transfers between devices, body(): lax.psum_scatter(broadcast_rows, 'leaf', scatter_dimension=0, tiled=True)  362 us
    dot_general x1, matrix products, body(): jnp.einsum('ug,ubc->gbc', table, blocks, precision=topmost_front)  58 us
    dot_general x1, local copies, waits for them, and re-layouts, body(): jnp.einsum('ug,ubc->gbc', table, blocks, precision=topmost_front)  56.5 us
    dot_general x8, matrix products, body(): jnp.dot(update_blocks[:, step * panel:(step + 1) * panel], received_contr...  39.1 us
    dot_general x7, matrix products, body(): jnp.dot(lower[:, step * panel:(step + 1) * panel], received_contribution,...  23.3 us
  transfers between devices with their start and end apart: 9, of which 9 were waited for; matrix products, arithmetic and copies ran while one was open for 3% of the time, Pallas kernels for 0%

commit v1 on v0

v1 whole, which is shorter than its diff:
```python
import jax
import jax.numpy as jnp
from jax import lax
from jax.experimental import pallas as pl
from jax.experimental.pallas import tpu as pltpu
from jax.sharding import PartitionSpec as P

BLK = 128
CW = 128
F32 = jnp.float32
BF16 = jnp.bfloat16
MESH = pl.DeviceIdType.MESH


def split(value):
    high = value.astype(BF16)
    return high, (value - high.astype(F32)).astype(BF16)


def product(left_high, left_low, right):
    right_high, right_low = split(right)
    n = right.shape[1]
    both = jnp.dot(
        left_high, jnp.concatenate([right_high, right_low], axis=1), preferred_element_type=F32
    )
    cross = jnp.dot(left_low, right_high, preferred_element_type=F32)
    return both[:, :n] + (both[:, n:] + cross)


def kernel(
    meta_ref, rhs_hbm, low_hbm, dinv_hbm, upd_hbm, ancr_hbm, anci_hbm,
    sol_out, anc_out,
    rhs_v, low_v, dinv_v, raw_v, ancr_v, anci_v,
    dh, dl, wh, wl, uh, ul, ah, al,
    acc_v, sol_v, upd_v, held, part, total, near_p, near_m, far_p, far_m, metas, table,
    rhs_sem, low_sem, dinv_sem, upd_sem, ancr_sem, anci_sem, meta_sem, sol_sem, anc_sem,
    panel_recv, own_send, fwd_send, relay_send,
    z1_send, z1_recv, x_send, x_recv, z2_send, z2_recv, mz_send, mz_recv, mx_send, mx_recv,
):
    chunks = sol_v.shape[0]
    leaf, row = lax.axis_index("leaf"), lax.axis_index("row")
    x, z = leaf // 4, lax.rem(leaf, 4)
    y, core = row // 2, lax.rem(row, 2)
    xp, xo, xm = (lax.rem(x + i, 4) for i in (1, 2, 3))
    zp, zo, zm = (lax.rem(z + i, 4) for i in (1, 2, 3))
    yp, ym = lax.rem(y + 1, 4), lax.rem(y + 3, 4)

    def device(xx, zz, rr):
        return {"leaf": xx * 4 + zz, "row": rr}

    sibling = device(x, z, y * 2 + 1 - core)
    to_yp, to_ym = device(x, z, yp * 2 + 1 - core), device(x, z, ym * 2 + 1 - core)
    to_zp, to_zo, to_zm = (device(x, i, row) for i in (zp, zo, zm))
    to_xp, to_xo, to_xm = (device(i, z, row) for i in (xp, xo, xm))

    def remote(src, dst, send, recv, to):
        return pltpu.make_async_remote_copy(
            src_ref=src, dst_ref=dst, send_sem=send, recv_sem=recv, device_id=to, device_id_type=MESH
        )

    def lanes(c):
        return pl.ds(pl.multiple_of(c * CW, CW), CW)

    load_dinv = pltpu.make_async_copy(dinv_hbm, dinv_v, dinv_sem)
    load_upd = pltpu.make_async_copy(upd_hbm, raw_v, upd_sem)
    load_anci = pltpu.make_async_copy(anci_hbm, anci_v, anci_sem)

    def load_rhs(c):
        return pltpu.make_async_copy(rhs_hbm.at[:, lanes(c)], rhs_v.at[c], rhs_sem.at[c])

    def load_ancr(c):
        return pltpu.make_async_copy(ancr_hbm.at[:, lanes(c)], ancr_v.at[c], ancr_sem.at[c])

    def load_low(k):
        columns = pl.ds(pl.multiple_of(k * 256, 256), 256)
        return pltpu.make_async_copy(low_hbm.at[:, columns], low_v.at[k], low_sem.at[k])

    def store_sol(c):
        return pltpu.make_async_copy(sol_v.at[c, row], sol_out.at[:, lanes(c)], sol_sem.at[c])

    def store_anc(c):
        return pltpu.make_async_copy(ancr_v.at[c], anc_out.at[:, lanes(c)], anc_sem.at[c])

    def own_copy(c, i):
        place = sol_v.at[c, row]
        return remote(
            place, place, own_send.at[i, c], panel_recv.at[row, c], (sibling, to_yp, to_ym)[i]
        )

    def forward(c, k, i):
        place = sol_v.at[c, k]
        return remote(place, place, fwd_send.at[i, c], panel_recv.at[k, c], sibling)

    def relay(c, k):
        place = sol_v.at[c, k]
        return remote(place, place, relay_send.at[c], panel_recv.at[k, c], to_yp)

    def arrive(c, k):
        owner_core = lax.rem(k, 2)
        away = lax.rem(y - k // 2 + 4, 4)
        forward(c, k, 0).wait_recv()
        crossed = owner_core == 1 - core
        straight = owner_core == core

        @pl.when((away == 1) & crossed)
        def _():
            relay(c, k).start()
            forward(c, k, 0).start()

        @pl.when((away == 2) & straight)
        def _():
            forward(c, k, 1).start()

        @pl.when((away == 3) & crossed)
        def _():
            forward(c, k, 2).start()

    def z1(c, i):
        if i == 0:
            src, dst, to = upd_v.at[c, pl.ds(128 * zp, 128)], held.at[c, pl.ds(512 * x + 128 * z, 128)], to_zp
        elif i == 1:
            src, dst, to = upd_v.at[c, pl.ds(128 * zm, 128)], held.at[c, pl.ds(512 * x + 128 * z, 128)], to_zm
        elif i == 2:
            src, dst, to = upd_v.at[c, pl.ds(128 * zo, 64)], near_p.at[c], to_zp
        elif i == 3:
            src, dst, to = upd_v.at[c, pl.ds(128 * zo + 64, 64)], near_m.at[c], to_zm
        elif i == 4:
            src, dst, to = near_p.at[c], held.at[c, pl.ds(512 * x + 128 * zm, 64)], to_zp
        else:
            src, dst, to = near_m.at[c], held.at[c, pl.ds(512 * x + 128 * zp + 64, 64)], to_zm
        return remote(src, dst, z1_send.at[i, c], z1_recv.at[i, c], to)

    def xc(c, i):
        if i == 0:
            place, to = held.at[c, pl.ds(512 * x, 512)], to_xp
        elif i == 1:
            place, to = held.at[c, pl.ds(512 * x, 512)], to_xm
        elif i == 2:
            place, to = held.at[c, pl.ds(512 * xm, 256)], to_xp
        else:
            place, to = held.at[c, pl.ds(512 * xp + 256, 256)], to_xm
        return remote(place, place, x_send.at[i, c], x_recv.at[i, c], to)

    def z2(c, i):
        if i == 0:
            src, dst, to = part.at[c, pl.ds(256 * zp, 256)], total.at[c, pl.ds(256 * z, 256)], to_zp
        elif i == 1:
            src, dst, to = part.at[c, pl.ds(256 * zm, 256)], total.at[c, pl.ds(256 * z, 256)], to_zm
        elif i == 2:
            src, dst, to = part.at[c, pl.ds(256 * zo, 128)], far_p.at[c], to_zp
        elif i == 3:
            src, dst, to = part.at[c, pl.ds(256 * zo + 128, 128)], far_m.at[c], to_zm
        elif i == 4:
            src, dst, to = far_p.at[c], total.at[c, pl.ds(256 * zm, 128)], to_zp
        else:
            src, dst, to = far_m.at[c], total.at[c, pl.ds(256 * zp + 128, 128)], to_zm
        return remote(src, dst, z2_send.at[i, c], z2_recv.at[i, c], to)

    def mz(i):
        return remote(
            meta_ref, metas.at[x, z], mz_send.at[i], mz_recv.at[i], (to_zp, to_zo, to_zm)[i]
        )

    def mx(i):
        return remote(
            metas.at[x], metas.at[x], mx_send.at[i], mx_recv.at[i], (to_xp, to_xo, to_xm)[i]
        )

    own_meta = pltpu.make_async_copy(meta_ref, metas.at[x, z], meta_sem)

    load_dinv.start()
    load_rhs(0).start()

    @pl.loop(0, row)
    def _(k):
        load_low(k).start()

    @pl.loop(1, chunks)
    def _(c):
        load_rhs(c).start()

    load_upd.start()
    load_anci.start()

    @pl.loop(0, chunks)
    def _(c):
        load_ancr(c).start()

    barrier = pltpu.get_barrier_semaphore()
    partners = (sibling, to_yp, to_ym, to_zp, to_zo, to_zm, to_xp, to_xo, to_xm)
    for to in partners:
        pl.semaphore_signal(barrier, inc=1, device_id=to, device_id_type=MESH)
    pl.semaphore_wait(barrier, len(partners))

    own_meta.start()
    for i in range(3):
        mz(i).start()

    load_dinv.wait()
    high, low = split(dinv_v[...])
    dh[...] = high
    dl[...] = low

    @pl.loop(0, row)
    def _(k):
        load_low(k).wait()
        high, low = split(product(dh[...], dl[...], low_v[k]))
        wh[k] = high
        wl[k] = low

    def split_update_rows():
        load_upd.wait()

        @pl.loop(0, 16)
        def _(q):
            source = pl.multiple_of(lax.rem(q, 4) * 128 + (q // 4) * 32, 32)
            target = pl.multiple_of(q * 32, 32)
            high, low = split(raw_v[pl.ds(source, 32), :])
            uh[pl.ds(target, 32), :] = high
            ul[pl.ds(target, 32), :] = low

    pl.when(y > 0)(split_update_rows)

    def solve(c):
        load_rhs(c).wait()
        acc_v[...] = product(dh[...], dl[...], rhs_v[c])

        @pl.loop(0, row)
        def _(k):
            arrive(c, k)
            acc_v[...] -= product(wh[k], wl[k], sol_v[c, k])

        sol_v[c, row] = acc_v[...]
        for i in range(3):
            own_copy(c, i).start()
        store_sol(c).start()

    def update(c):
        @pl.loop(row + 1, 8)
        def _(k):
            arrive(c, k)

        upd_v[c] = product(uh[...], ul[...], sol_v[c].reshape(2048, CW))
        held[c, pl.ds(pl.multiple_of(512 * x + 128 * z, 128), 128), :] = upd_v[
            c, pl.ds(pl.multiple_of(128 * z, 128), 128), :
        ]
        for i in (2, 3, 0, 1):
            z1(c, i).start()

    def meta_over_z():
        own_meta.wait()
        for i in range(3):
            mz(i).wait_recv()
        for i in range(3):
            mx(i).start()

    def make_table():
        for i in range(3):
            mx(i).wait_recv()
        meta = jnp.sum(metas[...].reshape(16, 8, 128), axis=0)
        wanted = (lax.broadcasted_iota(jnp.int32, (32, 128), 0) + (32 * x + 1)).astype(F32)
        row0 = jnp.broadcast_to(meta[0:1, :], (32, 128))
        table[...] = jnp.where(row0 == wanted, 1.0, 0.0).astype(BF16)
        anci = anci_v[...]
        high, low = split(anci)
        ah[...] = high
        al[...] = low

    def reduce(c):
        @pl.loop(0, 8)
        def _(g):
            for i in range(4):
                r = g * 4 + i
                pieces = held[c, pl.ds(r, 64, stride=32), :]
                high, low = split(pieces)
                part[c, pl.ds(r, 32, stride=32), :] = jnp.dot(
                    table[...], jnp.concatenate([high, low], axis=0), preferred_element_type=F32
                )

        own = pl.ds(pl.multiple_of(256 * z, 256), 256)
        total[c, own, :] = part[c, own, :]
        for i in (2, 3, 0, 1):
            z2(c, i).start()

    def ancestors(c):
        load_ancr(c).wait()
        for slot in range(8):
            rows = pl.ds(slot * 128, 128)
            summed = jnp.concatenate(
                [total[c, pl.ds(i * 256 + slot * 32, 32), :] for i in range(4)], axis=0
            )
            ancr_v[c, rows, :] = product(ah[rows, :], al[rows, :], ancr_v[c, rows, :] - summed)
        store_anc(c).start()

    ahead = 3 - y

    @pl.loop(0, chunks + 3 + ahead)
    def _(t):
        c0 = t - ahead
        c1, c2, c3 = c0 - 1, c0 - 2, c0 - 3

        def valid(c):
            return (c >= 0) & (c < chunks)

        @pl.when(valid(c1))
        def _():
            z1(c1, 2).wait_recv()
            z1(c1, 4).start()
            z1(c1, 3).wait_recv()
            z1(c1, 5).start()

        @pl.when(valid(c2))
        def _():
            xc(c2, 0).wait_recv()
            xc(c2, 2).start()
            xc(c2, 1).wait_recv()
            xc(c2, 3).start()

        @pl.when(valid(c3))
        def _():
            z2(c3, 2).wait_recv()
            z2(c3, 4).start()
            z2(c3, 3).wait_recv()
            z2(c3, 5).start()

        @pl.when(t < chunks)
        def _():
            solve(t)

        @pl.when(t == 0)
        def _():
            meta_over_z()
            pl.when(y == 0)(split_update_rows)

        @pl.when(valid(c0))
        def _():
            update(c0)

        @pl.when(valid(c1))
        def _():
            for i in (0, 1, 4, 5):
                z1(c1, i).wait_recv()
            xc(c1, 0).start()
            xc(c1, 1).start()

        @pl.when(c2 == 0)
        def _():
            load_anci.wait()
            make_table()

        @pl.when(valid(c2))
        def _():
            xc(c2, 2).wait_recv()
            xc(c2, 3).wait_recv()
            reduce(c2)

        @pl.when(valid(c3))
        def _():
            for i in (0, 1, 4, 5):
                z2(c3, i).wait_recv()
            ancestors(c3)

    for i in range(3):
        mz(i).wait_send()
        mx(i).wait_send()

    @pl.loop(0, chunks)
    def _(c):
        for i in range(3):
            own_copy(c, i).wait_send()
            forward(c, 0, i).wait_send()
        relay(c, 0).wait_send()
        for i in range(6):
            z1(c, i).wait_send()
            z2(c, i).wait_send()
        for i in range(4):
            xc(c, i).wait_send()
        store_sol(c).wait()
        store_anc(c).wait()


def body(
    right_side,
    lower_rows,
    diag_inverse,
    update_rows,
    owner_map,
    block_counts,
    ancestor_rhs,
    ancestor_inverse,
):
    leaf, row = lax.axis_index("leaf"), lax.axis_index("row")
    nblocks = owner_map.shape[1]
    columns = right_side.shape[2]
    chunks = columns // CW
    lane = lax.rem(jnp.arange(128, dtype=jnp.int32), 64)
    block = lax.rem(lane, nblocks)
    live = (lane // nblocks == leaf) & (row * nblocks + block < block_counts[0])
    owners = jnp.zeros((128,), jnp.int32)
    for j in range(nblocks):
        owners = jnp.where(block == j, owner_map[0, j], owners)
    meta = jnp.where(live, owners + 1, 0).astype(F32)
    meta = jnp.broadcast_to(meta[None], (8, 128))

    dma = pltpu.SemaphoreType.DMA
    vmem = pltpu.VMEM
    scratch = [
        vmem((chunks, 256, CW), F32),
        vmem((8, 256, 256), F32),
        vmem((256, 256), F32),
        vmem((512, 2048), F32),
        vmem((chunks, 1024, CW), F32),
        vmem((1024, 128), F32),
        vmem((256, 256), BF16),
        vmem((256, 256), BF16),
        vmem((8, 256, 256), BF16),
        vmem((8, 256, 256), BF16),
        vmem((512, 2048), BF16),
        vmem((512, 2048), BF16),
        vmem((1024, 128), BF16),
        vmem((1024, 128), BF16),
        vmem((256, CW), F32),
        vmem((chunks, 8, 256, CW), F32),
        vmem((chunks, 512, CW), F32),
        vmem((chunks, 2048, CW), F32),
        vmem((chunks, 1024, CW), F32),
        vmem((chunks, 1024, CW), F32),
        vmem((chunks, 64, CW), F32),
        vmem((chunks, 64, CW), F32),
        vmem((chunks, 128, CW), F32),
        vmem((chunks, 128, CW), F32),
        vmem((4, 4, 8, 128), F32),
        vmem((32, 128), BF16),
        dma((chunks,)),
        dma((8,)),
        dma,
        dma,
        dma((chunks,)),
        dma,
        dma,
        dma((chunks,)),
        dma((chunks,)),
        dma((8, chunks)),
        dma((3, chunks)),
        dma((3, chunks)),
        dma((chunks,)),
        dma((6, chunks)),
        dma((6, chunks)),
        dma((4, chunks)),
        dma((4, chunks)),
        dma((6, chunks)),
        dma((6, chunks)),
        dma((3,)),
        dma((3,)),
        dma((3,)),
        dma((3,)),
    ]
    anywhere = pl.BlockSpec(memory_space=pl.ANY)
    sol, anc = pl.pallas_call(
        kernel,
        out_shape=(
            jax.ShapeDtypeStruct((256, columns), F32),
            jax.ShapeDtypeStruct((1024, columns), F32),
        ),
        in_specs=[pl.BlockSpec(memory_space=pltpu.VMEM)] + [anywhere] * 6,
        out_specs=(anywhere, anywhere),
        scratch_shapes=scratch,
        compiler_params=pltpu.CompilerParams(
            collective_id=0, has_side_effects=True, vmem_limit_bytes=67043328
        ),
    )(
        meta,
        right_side[0],
        lower_rows[0],
        diag_inverse[0],
        update_rows[0],
        ancestor_rhs[0],
        ancestor_inverse[0],
    )
    return sol[None], anc[None]


def solution(mesh):
    in_specs = (
        P("leaf", "row", None),
        P("leaf", "row", None),
        P("leaf", "row", None),
        P("leaf", "row", None),
        P("leaf", "row"),
        P("leaf"),
        P("leaf", "row", None),
        P("leaf", "row", None),
    )
    out_specs = (P("leaf", "row", None), P("leaf", "row", None))
    return jax.shard_map(body, mesh=mesh, in_specs=in_specs, out_specs=out_specs, check_vma=False)
```

time: 1070 us -> 195 us (0.18); the launches traced: 1060 us -> 194 us
  waiting for transfers between devices: 828 us -> 0 us
  Pallas kernels: 0 us -> 181 us
  matrix products: 148 us -> 0 us
  local copies, waits for them, and re-layouts: 61.7 us -> 9.15 us
  between operations: 15 us -> 1.3 us
    psum x8 -> x0, waiting for transfers between devices: 465 us -> none  [spread(): return lax.psum(kept, axis)]
    reduce_scatter x1 -> x0, waiting for transfers between devices: 362 us -> none  [body(): lax.psum_scatter(broadcast_rows, 'leaf', scatter_dimension=0, tiled=True)]
    pallas_call x0 -> x1, Pallas kernels: none -> 181 us  [body(): pl.pallas_call(kernel, out_shape=(jax.ShapeDtypeStruct((256, columns), F3...]
    dot_general x25 -> x0, matrix products: 148 us -> none  [the longest x1 58 us: body(): jnp.einsum('ug,ubc->gbc', table, blocks, precision=topmost_front)]
    dot_general x1 -> x0, local copies, waits for them, and re-layouts: 56.5 us -> none  [body(): jnp.einsum('ug,ubc->gbc', table, blocks, precision=topmost_front)]
  transfers between devices with their start and end apart: 9 -> 0, of which waited for: 9 -> 0; matrix products, arithmetic and copies ran while one was open for 3% -> 0% of each run, Pallas kernels for 0% -> 0%
where the time goes in v1:
time: 195 us; the launch traced here: 194 us
  Pallas kernels  181 us (93%)
  local copies, waits for them, and re-layouts  9.15 us (5%)
  other arithmetic  2.57 us (1%)
    pallas_call x1, Pallas kernels, body(): pl.pallas_call(kernel, out_shape=(jax.ShapeDtypeStruct((256, columns), F3...  181 us
    unnamed x2, local copies, waits for them, and re-layouts  7.09 us

profile of v1, /device:TPU:8, one launch (start us, length us, event | category | flops | bytes accessed | tf_op | source)
XLA Modules:
  0.0 194.2 jit_solution(10259713209435210318)
XLA Ops:
  1.3 1.5 fusion.2
  2.7 2.6 %fusion.1 = f32[128]{0:T(128)S(1)} fusion(s32[]{:T(128)} %bitcast.4, s32[]{:T(128)} %bitcast.3, s32[]{:T(128)} %bitcast.2, s32[]{:T(128)} %bitcast.1, s32[]{:T(128)} %bitcast.13, s32[]{:T(128)S(6)} %mul.3, s32[]{:T(128)S(6)} %axis_index.23), kind=kLoop, calls=%fused_computation.10 | loop fusion | flops 3968 | bytes 540 | tf_op jit(solution)/shard_map/convert_element_type | solution.py:402
  5.3 0.6 broadcast_in_dim.31.meta_ref
  5.9 181.2 %shard_map.95 = (f32[256,1024]{1,0:T(8,128)}, f32[1024,1024]{1,0:T(8,128)}) custom-call(f32[8,128]{1,0:T(8,128)} %broadcast_in_dim.31.meta_ref, f32[256,1024]{1,0:T(8,128)} %bitcast.19, f32[256,2048]{1,0:T(8,128)} %bitcast.17, f32[256,256]{1,0:T(8,128)} %bitcast.21, f32[512,2048]{1,0:T(8,128)} %bitcast.14, f32[1024,1024]{1,0:T(8,128)} %bitcast.15, ...), custom_call_target="tpu_custom_call" | custom-call | tf_op jit(solution)/shard_map/pallas_call | solution.py:459
  187.1 2.3 %copy.13 = f32[1,256,1024]{2,1,0:T(8,128)} copy(f32[1,256,1024]{2,1,0:T(8,128)} %bitcast.18) | data formatting | bytes 2097152
  189.4 4.8 %copy.14 = f32[1,1024,1024]{2,1,0:T(8,128)} copy(f32[1,1024,1024]{2,1,0:T(8,128)} %bitcast.16) | data formatting | bytes 8388608

commit v2 on v1

v2 whole, which is shorter than its diff:
```python
import jax
import jax.numpy as jnp
from jax import lax
from jax.experimental import pallas as pl
from jax.experimental.pallas import tpu as pltpu
from jax.sharding import PartitionSpec as P

BLK = 128
CW = 128
AHEAD = (8, 5, 3, 1)
LAST_Y = 3
STAGES = (0, 1, 2, 3)
F32 = jnp.float32
BF16 = jnp.bfloat16
MESH = pl.DeviceIdType.MESH


def split(value):
    high = value.astype(BF16)
    return high, (value - high.astype(F32)).astype(BF16)


def product(left_high, left_low, right):
    right_high, right_low = split(right)
    n = right.shape[1]
    both = jnp.dot(
        left_high, jnp.concatenate([right_high, right_low], axis=1), preferred_element_type=F32
    )
    cross = jnp.dot(left_low, right_high, preferred_element_type=F32)
    return both[:, :n] + (both[:, n:] + cross)


def kernel(
    owner_ref, count_ref, rhs_hbm, low_hbm, dinv_hbm, upd_hbm, ancr_hbm, anci_hbm,
    sol_out, anc_out,
    rhs_v, low_v, dinv_v, raw_v, ancr_v, anci_v,
    dh, dl, wh, wl, uh, ul, ah, al,
    acc_v, sol_v, upd_v, held, part, total, meta_ref, metas, table,
    rhs_sem, low_sem, dinv_sem, upd_sem, ancr_sem, anci_sem, meta_sem, sol_sem, anc_sem,
    panel_recv, own_send, fwd_send,
    cut_send, cut_recv, ring_send, ring_recv, sum_send, sum_recv, mz_send, mz_recv, mx_send, mx_recv,
):
    chunks = sol_v.shape[0]
    leaf, row = lax.axis_index("leaf"), lax.axis_index("row")
    x, z = leaf // 4, lax.rem(leaf, 4)
    y, core = row // 2, lax.rem(row, 2)
    yp, ym = lax.rem(y + 1, 4), lax.rem(y + 3, 4)

    def device(xx, zz, rr):
        return {"leaf": xx * 4 + zz, "row": rr}

    sibling = device(x, z, y * 2 + 1 - core)
    to_yp, to_ym = device(x, z, yp * 2 + 1 - core), device(x, z, ym * 2 + 1 - core)
    to_yo = device(x, z, lax.rem(y + 2, 4) * 2 + core)
    to_z = [device(x, lax.rem(z + i, 4), row) for i in (1, 2, 3)]
    to_x = [device(lax.rem(x + i, 4), z, row) for i in (1, 2, 3)]
    cut_at, cut_to = (z, x), (to_z, to_x)
    ring_at, ring_to = (x, z), (to_x, to_z)

    def remote(src, dst, send, recv, to):
        return pltpu.make_async_remote_copy(
            src_ref=src, dst_ref=dst, send_sem=send, recv_sem=recv, device_id=to, device_id_type=MESH
        )

    def lanes(c):
        return pl.ds(pl.multiple_of(c * CW, CW), CW)

    def rows(start, size):
        return pl.ds(pl.multiple_of(start, size), size)

    load_dinv = pltpu.make_async_copy(dinv_hbm, dinv_v, dinv_sem)
    load_upd = pltpu.make_async_copy(upd_hbm, raw_v, upd_sem)
    load_anci = pltpu.make_async_copy(anci_hbm, anci_v, anci_sem)

    def load_rhs(c):
        return pltpu.make_async_copy(rhs_hbm.at[:, lanes(c)], rhs_v.at[c], rhs_sem.at[c])

    def load_ancr(c):
        return pltpu.make_async_copy(ancr_hbm.at[:, lanes(c)], ancr_v.at[c], ancr_sem.at[c])

    def load_low(k):
        columns = pl.ds(pl.multiple_of(k * 256, 256), 256)
        return pltpu.make_async_copy(low_hbm.at[:, columns], low_v.at[k], low_sem.at[k])

    def store_sol(c):
        return pltpu.make_async_copy(sol_v.at[c, row], sol_out.at[:, lanes(c)], sol_sem.at[c])

    def store_anc(c):
        return pltpu.make_async_copy(ancr_v.at[c], anc_out.at[:, lanes(c)], anc_sem.at[c])

    def own_copy(c, i):
        place = sol_v.at[c, row]
        return remote(
            place, place, own_send.at[i, c], panel_recv.at[row, c], (sibling, to_yp, to_ym, to_yo)[i]
        )

    def forward(c, k, i):
        place = sol_v.at[c, k]
        return remote(place, place, fwd_send.at[i, c], panel_recv.at[k, c], sibling)

    def route(k):
        away = lax.rem(y - k // 2 + 4, 4)
        same = lax.rem(k, 2) == core
        return away, ((away == 2) & same) | ((lax.rem(away, 2) == 1) & jnp.logical_not(same))

    def take(c, k):
        away, direct = route(k)

        @pl.when(direct)
        def _():
            forward(c, k, 0).wait_recv()
            forward(c, k, away - 1).start()

    def need(c, k):
        _, direct = route(k)

        @pl.when(jnp.logical_not(direct))
        def _():
            forward(c, k, 0).wait_recv()

    def cut(o, c, i):
        there = lax.rem(cut_at[o] + 1 + i, 4)
        return remote(
            upd_v.at[c, rows(256 * o + 64 * there, 64)],
            held.at[c, rows(1024 * o + 256 * ring_at[o] + 64 * cut_at[o], 64)],
            cut_send.at[o, i, c], cut_recv.at[o, i, c], cut_to[o][i],
        )

    def ring(o, c, i):
        origin = lax.rem(ring_at[o] + (0, 0, 0, 0, 3, 1)[i], 4)
        half = (0, 1, 1, 0, 0, 1)[i]
        place = held.at[c, rows(1024 * o + 256 * origin + 128 * half, 128)]
        to = ring_to[o][(0, 0, 2, 2, 0, 2)[i]]
        return remote(place, place, ring_send.at[o, i, c], ring_recv.at[o, i, c], to)

    def summed(o, c, i):
        there = lax.rem(cut_at[o] + 1 + i, 4)
        return remote(
            part.at[c, rows(512 * o + 128 * there, 128)],
            total.at[c, rows(512 * o + 128 * cut_at[o], 128)],
            sum_send.at[o, i, c], sum_recv.at[o, i, c], cut_to[o][i],
        )

    def mz(i):
        return remote(meta_ref, metas.at[x, z], mz_send.at[i], mz_recv.at[i], to_z[i])

    def mx(i):
        return remote(metas.at[x], metas.at[x], mx_send.at[i], mx_recv.at[i], to_x[i])

    own_meta = pltpu.make_async_copy(meta_ref, metas.at[x, z], meta_sem)

    load_dinv.start()
    load_rhs(0).start()

    lane = lax.broadcasted_iota(jnp.int32, (8, 128), 1) & 63
    order = lax.broadcasted_iota(jnp.int32, (8, 128), 0)
    block, source = lane & 3, lane >> 2
    place = jnp.where(order == 0, source, ((source & 3) << 2) | (source >> 2))
    owner = jnp.zeros((8, 128), jnp.int32)
    for j in range(4):
        owner = jnp.where(block == j, owner_ref[j] + 1, owner)
    live = (place == leaf) & (order < 2) & (block + row * 4 < count_ref[0])
    meta_ref[...] = jnp.where(live, owner, 0).astype(F32)

    @pl.loop(0, row)
    def _(k):
        load_low(k).start()

    @pl.loop(1, chunks)
    def _(c):
        load_rhs(c).start()

    load_upd.start()
    load_anci.start()

    @pl.loop(0, chunks)
    def _(c):
        load_ancr(c).start()

    barrier = pltpu.get_barrier_semaphore()
    partners = [sibling, to_yp, to_ym, to_yo, *to_z, *to_x]
    for to in partners:
        pl.semaphore_signal(barrier, inc=1, device_id=to, device_id_type=MESH)
    pl.semaphore_wait(barrier, len(partners))

    own_meta.start()
    for i in range(3):
        mz(i).start()

    load_dinv.wait()
    high, low = split(dinv_v[...])
    dh[...] = high
    dl[...] = low

    @pl.loop(0, row)
    def _(k):
        load_low(k).wait()
        high, low = split(product(dh[...], dl[...], low_v[k]))
        columns = pl.ds(pl.multiple_of(lax.rem(k, 2) * 256, 256), 256)
        wh[k // 2, :, columns] = high
        wl[k // 2, :, columns] = low

    early = y <= 1

    def start_rhs(c):
        load_rhs(c).wait()
        rhs_v[c] = product(dh[...], dl[...], rhs_v[c])

    def split_update_rows():
        load_upd.wait()

        @pl.loop(0, 32)
        def _(q):
            source = lax.rem(q, 4) * 128 + (q // 16) * 64 + lax.rem(q // 4, 4) * 16
            high, low = split(raw_v[rows(source, 16), :])
            uh[rows(q * 16, 16), :] = high
            ul[rows(q * 16, 16), :] = low

    @pl.when(jnp.logical_not(early))
    def _():
        @pl.loop(0, chunks)
        def _(c):
            start_rhs(c)

        split_update_rows()

    def take_early(c):
        @pl.loop(0, row)
        def _(k):
            take(c, k)

    def take_late(c, start, stop):
        @pl.loop(jnp.maximum(row + 1, start), stop)
        def _(k):
            take(c, k)

    def solve(c):
        @pl.when(early)
        def _():
            start_rhs(c)

        acc_v[...] = rhs_v[c]

        @pl.loop(0, y)
        def _(j):
            @pl.when(c == 0)
            def _():
                take(c, 2 * j)
                take(c, 2 * j + 1)

            need(c, 2 * j)
            need(c, 2 * j + 1)
            acc_v[...] -= product(
                wh[j], wl[j], sol_v[c, pl.ds(2 * j, 2)].reshape(512, CW)
            )

        @pl.when(core == 1)
        def _():
            need(c, 2 * y)
            acc_v[...] -= product(wh[y, :, pl.ds(0, 256)], wl[y, :, pl.ds(0, 256)], sol_v[c, 2 * y])

        sol_v[c, row] = acc_v[...]
        for i in range(4):
            own_copy(c, i).start()
        store_sol(c).start()

    def update(c):
        @pl.loop(row + 1, 6)
        def _(k):
            need(c, k)

        first, last = pl.ds(0, 1536), pl.ds(1536, 512)
        upd_v[c] = product(uh[:, first], ul[:, first], sol_v[c, pl.ds(0, 6)].reshape(1536, CW))

        @pl.when(c == 0)
        def _():
            take_late(c, 6, 8)

        @pl.loop(jnp.maximum(row + 1, 6), 8)
        def _(k):
            need(c, k)

        upd_v[c] += product(uh[:, last], ul[:, last], sol_v[c, pl.ds(6, 2)].reshape(512, CW))
        for o in range(2):
            own = rows(1024 * o + 256 * ring_at[o] + 64 * cut_at[o], 64)
            held[c, own, :] = upd_v[c, rows(256 * o + 64 * cut_at[o], 64), :]
        for i in (1, 0, 2):
            for o in range(2):
                cut(o, c, i).start()

    def meta_over_z():
        own_meta.wait()
        for i in range(3):
            mz(i).wait_recv()
        for i in range(3):
            mx(i).start()

    def make_tables():
        load_anci.wait()
        high, low = split(anci_v[...])
        ah[...] = high
        al[...] = low
        for i in range(3):
            mx(i).wait_recv()
        meta = jnp.sum(metas[...].reshape(16, 8, 128), axis=0)
        target = lax.broadcasted_iota(jnp.int32, (32, 128), 0)
        wanted = (32 * x + target, target // 8 * 32 + 8 * z + lax.rem(target, 8))
        for o in range(2):
            sources = jnp.broadcast_to(meta[o : o + 1, :], (32, 128))
            table[o] = jnp.where(sources == (wanted[o] + 1).astype(F32), 1.0, 0.0).astype(BF16)

    def start_ring(c):
        for o in range(2):
            for i in range(3):
                cut(o, c, i).wait_recv()
            for i in (0, 2, 1, 3):
                ring(o, c, i).start()

    def pass_on(c):
        for o in range(2):
            for i in (0, 2):
                ring(o, c, i).wait_recv()
                ring(o, c, 4 + i // 2).start()

    def reduce(c):
        for o in range(2):
            for i in (1, 3, 4, 5):
                ring(o, c, i).wait_recv()

        @pl.loop(0, 2)
        def _(g):
            for i in range(8):
                for o in range(2):
                    r = g * 8 + i
                    pieces = held[c, pl.ds(1024 * o + r, 64, stride=16), :]
                    high, low = split(pieces)
                    part[c, pl.ds(512 * o + r, 32, stride=16), :] = jnp.dot(
                        table[o], jnp.concatenate([high, low], axis=0), preferred_element_type=F32
                    )

        for o in range(2):
            own = rows(512 * o + 128 * cut_at[o], 128)
            total[c, own, :] = part[c, own, :]
        for i in (1, 0, 2):
            for o in range(2):
                summed(o, c, i).start()

    def ancestors(c):
        for o in range(2):
            for i in range(3):
                summed(o, c, i).wait_recv()
        load_ancr(c).wait()
        for slot in range(8):
            here = pl.ds(slot * 128, 128)
            gone = jnp.concatenate(
                [total[c, pl.ds(i * 128 + slot * 16, 16), :] for i in range(8)], axis=0
            )
            ancr_v[c, here, :] = product(ah[here, :], al[here, :], ancr_v[c, here, :] - gone)
        store_anc(c).start()

    ahead = jnp.where(y == 0, AHEAD[0], jnp.where(y == 1, AHEAD[1], jnp.where(y == 2, AHEAD[2], AHEAD[3])))

    @pl.loop(0, chunks + ahead + STAGES[-1])
    def _(t):
        c0 = t - ahead

        def stage(k, work):
            c = c0 - STAGES[k]
            pl.when((c >= 0) & (c < chunks))(lambda: work(c))

        @pl.when(c0 == 0)
        def _():
            meta_over_z()
            pl.when(early)(split_update_rows)

        @pl.when((t > 0) & (t < chunks) & (y < LAST_Y))
        def _():
            take_early(t)

        @pl.when((c0 >= 0) & (c0 < chunks))
        def _():
            update(c0)

        @pl.when((t > 0) & (t < chunks) & (y >= LAST_Y))
        def _():
            take_early(t)

        @pl.when(t < chunks)
        def _():
            solve(t)

        stage(1, pass_on)

        @pl.when((c0 + 1 >= 0) & (c0 + 1 < chunks))
        def _():
            take_late(c0 + 1, 0, jnp.where(c0 + 1 == 0, 6, 8))

        @pl.when(c0 == 1)
        def _():
            make_tables()

        stage(2, reduce)
        stage(3, ancestors)
        stage(0, start_ring)

    for i in range(3):
        mz(i).wait_send()
        mx(i).wait_send()

    @pl.loop(0, chunks)
    def _(c):
        for i in range(4):
            own_copy(c, i).wait_send()
        for i in range(3):
            forward(c, 0, i).wait_send()
        for o in range(2):
            for i in range(3):
                cut(o, c, i).wait_send()
                summed(o, c, i).wait_send()
            for i in range(6):
                ring(o, c, i).wait_send()
        store_sol(c).wait()
        store_anc(c).wait()


def copy_kernel(sol_in, anc_in, sol_out, anc_out, buffer, load_sem, store_sem):
    loads, stores = [], []
    for i in range(10):
        source, target, j = (sol_in, sol_out, i) if i < 2 else (anc_in, anc_out, i - 2)
        here = pl.ds(j * 128, 128)
        loads.append(pltpu.make_async_copy(source.at[here], buffer.at[i], load_sem.at[i]))
        stores.append(pltpu.make_async_copy(buffer.at[i], target.at[here], store_sem.at[i]))
    for load in loads:
        load.start()
    for load, store in zip(loads, stores):
        load.wait()
        store.start()
    for store in stores:
        store.wait()


def body(
    right_side,
    lower_rows,
    diag_inverse,
    update_rows,
    owner_map,
    block_counts,
    ancestor_rhs,
    ancestor_inverse,
):
    columns = right_side.shape[2]
    chunks = columns // CW
    dma = pltpu.SemaphoreType.DMA
    vmem = pltpu.VMEM
    scratch = [
        vmem((chunks, 256, CW), F32),
        vmem((8, 256, 256), F32),
        vmem((256, 256), F32),
        vmem((512, 2048), F32),
        vmem((chunks, 1024, CW), F32),
        vmem((1024, 128), F32),
        vmem((256, 256), BF16),
        vmem((256, 256), BF16),
        vmem((4, 256, 512), BF16),
        vmem((4, 256, 512), BF16),
        vmem((512, 2048), BF16),
        vmem((512, 2048), BF16),
        vmem((1024, 128), BF16),
        vmem((1024, 128), BF16),
        vmem((256, CW), F32),
        vmem((chunks, 8, 256, CW), F32),
        vmem((chunks, 512, CW), F32),
        vmem((chunks, 2048, CW), F32),
        vmem((chunks, 1024, CW), F32),
        vmem((chunks, 1024, CW), F32),
        vmem((8, 128), F32),
        vmem((4, 4, 8, 128), F32),
        vmem((2, 32, 128), BF16),
        dma((chunks,)),
        dma((8,)),
        dma,
        dma,
        dma((chunks,)),
        dma,
        dma,
        dma((chunks,)),
        dma((chunks,)),
        dma((8, chunks)),
        dma((4, chunks)),
        dma((3, chunks)),
        dma((2, 3, chunks)),
        dma((2, 3, chunks)),
        dma((2, 6, chunks)),
        dma((2, 6, chunks)),
        dma((2, 3, chunks)),
        dma((2, 3, chunks)),
        dma((3,)),
        dma((3,)),
        dma((3,)),
        dma((3,)),
    ]
    anywhere = pl.BlockSpec(memory_space=pl.ANY)
    sol, anc = pl.pallas_call(
        kernel,
        out_shape=(
            jax.ShapeDtypeStruct((256, columns), F32),
            jax.ShapeDtypeStruct((1024, columns), F32),
        ),
        in_specs=[pl.BlockSpec(memory_space=pltpu.SMEM)] * 2 + [anywhere] * 6,
        out_specs=(anywhere, anywhere),
        scratch_shapes=scratch,
        compiler_params=pltpu.CompilerParams(
            collective_id=0, has_side_effects=True, vmem_limit_bytes=67043328
        ),
    )(
        owner_map[0],
        block_counts,
        right_side[0],
        lower_rows[0],
        diag_inverse[0],
        update_rows[0],
        ancestor_rhs[0],
        ancestor_inverse[0],
    )
    sol, anc = pl.pallas_call(
        copy_kernel,
        out_shape=(
            jax.ShapeDtypeStruct((256, columns), F32),
            jax.ShapeDtypeStruct((1024, columns), F32),
        ),
        in_specs=[anywhere] * 2,
        out_specs=(anywhere, anywhere),
        scratch_shapes=[vmem((10, 128, columns), F32), dma((10,)), dma((10,))],
        compiler_params=pltpu.CompilerParams(vmem_limit_bytes=67043328),
    )(sol, anc)
    return sol[None], anc[None]


def solution(mesh):
    in_specs = (
        P("leaf", "row", None),
        P("leaf", "row", None),
        P("leaf", "row", None),
        P("leaf", "row", None),
        P("leaf", "row"),
        P("leaf"),
        P("leaf", "row", None),
        P("leaf", "row", None),
    )
    out_specs = (P("leaf", "row", None), P("leaf", "row", None))
    return jax.shard_map(body, mesh=mesh, in_specs=in_specs, out_specs=out_specs, check_vma=False)
```

time: 195 us -> 131 us (0.67)
  Pallas kernels: 181 us -> 130 us
  local copies, waits for them, and re-layouts: 9.15 us -> 0 us
  other arithmetic: 2.57 us -> 0 us
    pallas_call x1, Pallas kernels: 181 us -> 125 us  [body(): pl.pallas_call(kernel, out_shape=(jax.ShapeDtypeStruct((256, columns), F3...]
    unnamed x2 -> x0, local copies, waits for them, and re-layouts: 7.09 us -> none
    pallas_call x0 -> x1, Pallas kernels: none -> 4.71 us  [body(): pl.pallas_call(copy_kernel, out_shape=(jax.ShapeDtypeStruct((256, columns...]
    convert_element_type x1 -> x0, other arithmetic: 2.57 us -> none  [body(): meta = jnp.where(live, owners + 1, 0).astype(F32)]
where the time goes in v2:
time: 131 us
  Pallas kernels  130 us (99%)
    pallas_call x1, Pallas kernels, body(): pl.pallas_call(kernel, out_shape=(jax.ShapeDtypeStruct((256, columns), F3...  125 us
    pallas_call x1, Pallas kernels, body(): pl.pallas_call(copy_kernel, out_shape=(jax.ShapeDtypeStruct((256, columns...  4.71 us

profile of v2, /device:TPU:8, one launch (start us, length us, event | category | flops | bytes accessed | tf_op | source)
XLA Modules:
  0.0 131.1 jit_solution(12622862391051302201)
XLA Ops:
  1.3 125.1 %shard_map.95 = (f32[256,1024]{1,0:T(8,128)}, f32[1024,1024]{1,0:T(8,128)}) custom-call(s32[4]{0:T(128)} %bitcast.15, s32[1]{0:T(128)S(6)} %copy.10.count_ref, f32[256,1024]{1,0:T(8,128)} %bitcast.12, f32[256,2048]{1,0:T(8,128)} %bitcast.11, f32[256,256]{1,0:T(8,128)} %bitcast.14, f32[512,2048]{1,0:T(8,128)} %bitcast.9, f32[1024,1024]{1,0:T(8,128)} %bitcast.10, ...), custom_call_target="tpu_custom_call" | custom-call | tf_op jit(solution)/shard_map/pallas_call | solution.py:504
  126.4 4.7 %shard_map.96 = (f32[256,1024]{1,0:T(8,128)}, f32[1024,1024]{1,0:T(8,128)}) custom-call(f32[256,1024]{1,0:T(8,128)} %get-tuple-element.6.sol_in, f32[1024,1024]{1,0:T(8,128)} %get-tuple-element.7.anc_in), custom_call_target="tpu_custom_call" | custom-call | tf_op jit(solution)/shard_map/pallas_call | solution.py:526

commit v3 on v2

--- a/solution.py
+++ b/solution.py
@@ -8,7 +8,7 @@
 BLK = 128
 CW = 128
 AHEAD = (8, 5, 3, 1)
-LAST_Y = 3
+LAST_Y = 1
 STAGES = (0, 1, 2, 3)
 F32 = jnp.float32
 BF16 = jnp.bfloat16
@@ -260,8 +260,19 @@
             acc_v[...] -= product(wh[y, :, pl.ds(0, 256)], wl[y, :, pl.ds(0, 256)], sol_v[c, 2 * y])
 
         sol_v[c, row] = acc_v[...]
-        for i in range(4):
-            own_copy(c, i).start()
+        own_copy(c, 0).start()
+
+        @pl.when(y == 3)
+        def _():
+            own_copy(c, 3).start()
+
+        own_copy(c, 1).start()
+        own_copy(c, 2).start()
+
+        @pl.when(y < 3)
+        def _():
+            own_copy(c, 3).start()
+
         store_sol(c).start()
 
     def update(c):
@@ -400,8 +411,8 @@
             make_tables()
 
         stage(2, reduce)
+        stage(0, start_ring)
         stage(3, ancestors)
-        stage(0, start_ring)
 
     for i in range(3):
         mz(i).wait_send()

time: 131 us -> 129 us (0.985)
  Pallas kernels: 130 us -> 128 us
    pallas_call x1, Pallas kernels: 125 us -> 123 us  [body(): pl.pallas_call(kernel, out_shape=(jax.ShapeDtypeStruct((256, columns), F3...]
where the time goes in v3:
time: 129 us
  Pallas kernels  128 us (99%)
  between operations  1.29 us (1%)
    pallas_call x1, Pallas kernels, body(): pl.pallas_call(kernel, out_shape=(jax.ShapeDtypeStruct((256, columns), F3...  123 us
    pallas_call x1, Pallas kernels, body(): pl.pallas_call(copy_kernel, out_shape=(jax.ShapeDtypeStruct((256, columns...  4.71 us

profile of v3, /device:TPU:8, one launch (start us, length us, event | category | flops | bytes accessed | tf_op | source)
XLA Modules:
  0.0 129.3 jit_solution(218782423505264673)
XLA Ops:
  1.3 123.3 %shard_map.95 = (f32[256,1024]{1,0:T(8,128)}, f32[1024,1024]{1,0:T(8,128)}) custom-call(s32[4]{0:T(128)} %bitcast.15, s32[1]{0:T(128)S(6)} %copy.10.count_ref, f32[256,1024]{1,0:T(8,128)} %bitcast.12, f32[256,2048]{1,0:T(8,128)} %bitcast.11, f32[256,256]{1,0:T(8,128)} %bitcast.14, f32[512,2048]{1,0:T(8,128)} %bitcast.9, f32[1024,1024]{1,0:T(8,128)} %bitcast.10, ...), custom_call_target="tpu_custom_call" | custom-call | tf_op jit(solution)/shard_map/pallas_call | solution.py:515
  124.6 4.7 %shard_map.96 = (f32[256,1024]{1,0:T(8,128)}, f32[1024,1024]{1,0:T(8,128)}) custom-call(f32[256,1024]{1,0:T(8,128)} %get-tuple-element.6.sol_in, f32[1024,1024]{1,0:T(8,128)} %get-tuple-element.7.anc_in), custom_call_target="tpu_custom_call" | custom-call | tf_op jit(solution)/shard_map/pallas_call | solution.py:537
